TPU v7x, 32 devices: a whole 2x2x4 slice. The times are simulated.
32 devices in a mesh: batch: 4 (over z), token: 8 (over y, x, core).
Axes of the slice: x: 2, y: 2, z: 4, core: 2. Of those that a mesh axis runs over, the one named last changes fastest.
Arguments:
- tokens: bfloat16 [16384, 768], P(('batch', 'token')), may hold values from -9 to 9
- slot_weight: bfloat16 [768, 1024], replicated, may hold values from -2 to 2
- expert_in: bfloat16 [128, 768, 3072], P('token', None, 'batch'), may hold values from -1.7265625 to 1.7265625
- expert_out: bfloat16 [128, 3072, 768], P('token', 'batch'), may hold values from -0.6484375 to 0.6484375
Outputs:
- mixed: bfloat16 [16384, 768], P(('batch', 'token'))
All inputs are finite; a program needn't handle non-finite values.
Results may differ from a plain program's by a relative error of at most 0.023.
Values may be sent and summed in bfloat16 or wider, within the bound.
No kernel may reach another device: no remote copies, remote signals or barrier semaphores. Data moves between devices by JAX's collectives and lax.ppermute only.
A program may use at most 128 MiB of HBM per device.

v0:
```python
import jax
import jax.numpy as jnp
from jax import lax
from jax.sharding import PartitionSpec as P


def body(tokens, slot_weight, expert_in, expert_out):
    widened = tokens.astype(jnp.float32)
    scale_row = lax.rsqrt(jnp.mean(widened * widened, axis=-1, keepdims=True) + 1e-06)
    normed = (widened * scale_row).astype(jnp.bfloat16)
    logits = jnp.dot(normed, slot_weight, preferred_element_type=jnp.float32)
    column_max = lax.pmax(jnp.max(logits, axis=0), "token")
    raised = jnp.exp(logits - column_max[None, :])
    column_sum = lax.psum(jnp.sum(raised, axis=0), "token")
    dispatch = raised.astype(jnp.bfloat16)
    partial_value = jnp.einsum("ts,td->sd", dispatch, normed, preferred_element_type=jnp.float32)
    own_count = slot_weight.shape[1] // lax.axis_size("token")
    offset = lax.axis_index("token") * own_count
    own_rows = lax.psum_scatter(
        partial_value.astype(jnp.bfloat16), "token", scatter_dimension=0, tiled=True
    ).astype(jnp.float32)
    own_total = lax.dynamic_slice_in_dim(column_sum, offset, own_count, 0)
    experts_here = expert_in.shape[0]
    slot_inputs = (own_rows / own_total[:, None]).astype(jnp.bfloat16)
    slot_inputs = slot_inputs.reshape(experts_here, own_count // experts_here, tokens.shape[1])
    hidden = jnp.einsum(
        "esd,edf->esf",
        lax.all_gather(slot_inputs, "batch", axis=1, tiled=True),
        expert_in,
        preferred_element_type=jnp.float32,
    )
    hidden = jax.nn.gelu(hidden, approximate=False).astype(jnp.bfloat16)
    terms = jnp.einsum("esf,efd->esd", hidden, expert_out, preferred_element_type=jnp.float32)
    slot_outputs = lax.psum_scatter(
        terms.astype(jnp.bfloat16), "batch", scatter_dimension=1, tiled=True
    )
    combine = jax.nn.softmax(logits, axis=1).astype(jnp.bfloat16)
    slots_each = slot_outputs.shape[1]
    block_rows = lax.all_gather(slot_outputs, "token", axis=0, tiled=True)
    number = block_rows.shape[0]
    flat_rows = block_rows.reshape(number * slots_each, block_rows.shape[2])
    mixed = jnp.dot(combine, flat_rows, preferred_element_type=jnp.float32)
    return mixed.astype(jnp.bfloat16)


def solution(mesh):
    placed = (
        P(("batch", "token"), None),
        P(),
        P("token", None, "batch"),
        P("token", "batch", None),
    )
    return jax.shard_map(
        body, mesh=mesh, in_specs=placed, out_specs=P(("batch", "token"), None), check_vma=False
    )
```

profile of v0, /device:TPU:0, one launch (start us, length us, event | category | flops | bytes accessed | tf_op | source)
XLA Modules:
  0.0 166.7 jit_solution(7911845399044545035)
XLA Ops:
  6.5 0.0 copy-start
  6.5 0.0 reduce-scatter.5.cloned.1.call-start
  6.5 1.5 fusion.3
  8.0 0.1 copy-done
  8.2 0.0 copy-start.1
  8.2 3.6 %fusion.93 = (f32[512]{0:T(512)S(1)}, f32[1024]{0:T(1024)S(1)}, f32[512,1024]{1,0:T(8,128)}) fusion(bf16[768,1024]{1,0:T(8,128)(2,1)S(1)} %copy-done, bf16[512,768]{1,0:T(8,128)(2,1)} %param.4, f32[512]{0:T(512)S(1)} %add_rsqrt_fusion), kind=kOutput, calls=%fused_computation.110 | convolution fusion | flops 807533056 | bytes 4464640 | tf_op jit(solution)/shard_map/dot_general | solution.py:11
  11.8 15.1 %pmax.7 = f32[1024]{0:T(1024)S(1)} all-reduce(f32[1024]{0:T(1024)S(1)} %get-tuple-element.8), channel_id=1, replica_groups=mesh['batch'=4,'token'=8] {'token'}, use_global_device_ids=true, to_apply=%region_4.0 | all-reduce | flops 1024 | bytes 8192 | tf_op jit(solution)/shard_map/pmax | solution.py:12
  26.9 0.0 copy-done.1
  26.9 3.9 %convolution_convert_fusion = bf16[1024,768]{1,0:T(8,128)(2,1)} fusion(f32[512,1024]{1,0:T(8,128)} %get-tuple-element.11, f32[1024]{0:T(1024)S(1)} %pmax.7, bf16[512,768]{1,0:T(8,128)(2,1)S(1)} %copy-done.1, f32[512]{0:T(512)S(1)} %add_rsqrt_fusion), kind=kOutput, calls=%fused_computation.9 | convolution fusion | flops 808321024 | bytes 4462592 | tf_op jit(solution)/shard_map/ts,td->sd/dot_general | solution.py:16
  30.8 0.0 reduce-scatter.5.cloned.1.call-update
  30.8 0.0 reduce-scatter.7.cloned.1.call-start
  30.8 2.3 %fusion = (f32[512]{0:T(512)S(1)}, f32[1024]{0:T(1024)S(1)}) fusion(f32[512,1024]{1,0:T(8,128)} %get-tuple-element.11, f32[512]{0:T(512)S(1)} %get-tuple-element.7, f32[1024]{0:T(1024)S(1)} %pmax.7), kind=kLoop, calls=%fused_computation.6 | loop fusion | flops 2095616 | bytes 2109440 | tf_op jit(solution)/shard_map/reduce_sum | solution.py:37
  33.1 11.8 %psum.7 = f32[1024]{0:T(1024)S(1)} all-reduce(f32[1024]{0:T(1024)S(1)} %get-tuple-element.6), channel_id=1, replica_groups=mesh['batch'=4,'token'=8] {'token'}, use_global_device_ids=true, to_apply=%region_7.0 | all-reduce | flops 1024 | bytes 8192 | tf_op jit(solution)/shard_map/psum | solution.py:14
  44.9 0.1 dynamic_slice.3
  45.0 23.6 %reduce-scatter.5.cloned.1.call-done = bf16[128,768]{1,0:T(8,128)(2,1)} async-done(((bf16[1024,768]{1,0:T(8,128)(2,1)}), bf16[128,768]{1,0:T(8,128)(2,1)}) %reduce-scatter.5.cloned.1.call-update) | async-done | bytes 196624 | tf_op jit(solution)/shard_map/reduce_scatter | solution.py:19
  68.7 1.0 fusion.61
  69.7 19.6 %all_gather.6 = bf16[16,32,768]{2,1,0:T(8,128)(2,1)S(1)} all-gather(bf16[16,8,768]{2,1,0:T(8,128)(2,1)S(1)} %fusion.61), channel_id=1, replica_groups=mesh['batch'=4,'token'=8] {'batch'}, dimensions={1}, use_global_device_ids=true | all-gather | bytes 983040 | tf_op jit(solution)/shard_map/all_gather | solution.py:28
  89.3 8.1 %fusion.55 = (u16[32,768]{1,0:T(8,128)(2,1)S(1)}, u16[32,768]{1,0:T(8,128)(2,1)S(1)}, f32[16,32,768]{2,1,0:T(8,128)S(1)}) fusion(bf16[16,32,768]{2,1,0:T(8,128)(2,1)S(1)} %all_gather.6, bf16[16,768,768]{2,1,0:T(8,128)(2,1)} %param.6), kind=kOutput, calls=%fused_computation.71 | convolution fusion | flops 609042432 | bytes 21331968 | tf_op jit(solution)/shard_map/esd,edf->esf/dot_general | solution.py:26
  97.4 9.0 %fusion.94 = bf16[4,8,16,768]{3,1,0,2:T(8,128)(2,1)S(1)} fusion(bf16[16,768,768]{2,1,0:T(8,128)(2,1)} %param.7, f32[16,32,768]{2,1,0:T(8,128)S(1)} %get-tuple-element.12, u16[32,768]{1,0:T(8,128)(2,1)S(1)} %get-tuple-element.10, u16[32,768]{1,0:T(8,128)(2,1)S(1)} %get-tuple-element.9), kind=kOutput, calls=%fused_computation.111 | convolution fusion | flops 631898112 | bytes 21331968 | tf_op jit(solution)/shard_map/esf,efd->esd/dot_general | solution.py:33
  106.5 0.9 copy.7
  107.4 0.0 reduce-scatter.7.cloned.1.call-update
  107.4 0.0 all-gather.2.cloned.1.call-start
  107.5 21.8 %reduce-scatter.7.cloned.1.call-done = bf16[8,12288]{1,0:T(8,128)(2,1)} async-done(((bf16[32,12288]{1,0:T(8,128)(2,1)}), bf16[8,12288]{1,0:T(8,128)(2,1)}) %reduce-scatter.7.cloned.1.call-update) | async-done | bytes 196624
  129.2 1.0 copy.11
  130.2 0.7 copy.6
  130.9 0.0 all-gather.2.cloned.1.call-update
  131.0 25.3 %all-gather.2.cloned.1.call-done = bf16[128,8,768]{2,1,0:T(8,128)(2,1)} async-done(((bf16[16,8,768]{2,1,0:T(8,128)(2,1)}), bf16[128,8,768]{2,1,0:T(8,128)(2,1)}) %all-gather.2.cloned.1.call-update) | async-done | bytes 1572880 | tf_op jit(solution)/shard_map/all_gather | solution.py:39
  156.2 4.0 %fusion.16 = bf16[512,768]{1,0:T(8,128)(2,1)} fusion(bf16[128,8,768]{2,1,0:T(8,128)(2,1)} %all-gather.2.cloned.1.call-done, f32[512,1024]{1,0:T(8,128)} %get-tuple-element.11, f32[512]{0:T(512)S(1)} %get-tuple-element.5, f32[512]{0:T(512)S(1)} %get-tuple-element.7), kind=kOutput, calls=%fused_computation.35 | convolution fusion | flops 807272448 | bytes 4460544 | tf_op jit(solution)/shard_map/dot_general | solution.py:42
  (1 shorter events, 0.0 us)
Async XLA Ops:
  6.5 1.6 copy-start
  6.5 62.1 %reduce-scatter.5.cloned.1.call-start = ((), (), s32[]{:S(2)}) async-start(), calls=%async_computation.2 | async-start | bytes 1769472 | tf_op jit(solution)/shard_map/reduce_scatter | solution.py:19
  8.2 18.7 %copy-start.1 = (bf16[512,768]{1,0:T(8,128)(2,1)S(1)}, bf16[512,768]{1,0:T(8,128)(2,1)}, u32[]{:S(2)}) copy-start(bf16[512,768]{1,0:T(8,128)(2,1)} %param.4) | copy-start | bytes 2359300
  30.8 98.4 %reduce-scatter.7.cloned.1.call-start = ((), (), s32[]{:S(2)}) async-start(), calls=%async_computation.4 | async-start | bytes 983040
  107.4 48.8 %all-gather.2.cloned.1.call-start = ((), (), s32[]{:S(2)}) async-start(), calls=%async_computation.3 | async-start | bytes 1769472 | tf_op jit(solution)/shard_map/all_gather | solution.py:39
Sparse Core Ops, SparseCore 0:
  30.9 37.7 reduce-scatter.4
  107.5 21.6 reduce-scatter.6
  131.1 25.0 all-gather.1
where the time goes:
time: 167 us
  waiting for transfers between devices  70.7 us (42%)
  blocking collectives  46.5 us (28%)
  matrix products  28.6 us (17%)
  between operations  13.1 us (8%)
  other arithmetic  4.83 us (3%)
  local copies, waits for them, and re-layouts  2.86 us (2%)
    all_gather x1, waiting for transfers between devices, body(): block_rows = lax.all_gather(slot_outputs, 'token', axis=0, tiled=True)  25.3 us
    reduce_scatter x1, waiting for transfers between devices, body(): lax.psum_scatter(partial_value.astype(jnp.bfloat16), 'token', scatter_dim...  23.6 us
    unnamed x4, waiting for transfers between devices  21.8 us
    all_gather x1, blocking collectives, body(): lax.all_gather(slot_inputs, 'batch', axis=1, tiled=True)  19.6 us
    pmax x1, blocking collectives, body(): column_max = lax.pmax(jnp.max(logits, axis=0), 'token')  15.1 us
    psum x1, blocking collectives, body(): column_sum = lax.psum(jnp.sum(raised, axis=0), 'token')  11.8 us
    dot_general x1, matrix products, body(): jnp.einsum('esf,efd->esd', hidden, expert_out, preferred_element_type=jnp...  9.04 us
    dot_general x1, matrix products, body(): jnp.einsum('esd,edf->esf', lax.all_gather(slot_inputs, 'batch', axis=1, t...  8.12 us
  transfers between devices with their start and end apart: 3, of which 3 were waited for; matrix products, arithmetic and copies ran while one was open for 1% of the time, Pallas kernels for 0%

commit v1 on v0

--- a/solution.py
+++ b/solution.py
@@ -2,6 +2,32 @@
 import jax.numpy as jnp
 from jax import lax
 from jax.sharding import PartitionSpec as P
+
+
+def on_each_block(x, axis, dim, work, out_dim):
+    devices, here, rows = (lax.axis_size(axis), lax.axis_index(axis), x.shape[dim])
+    ahead = [(i, (i + 1) % devices) for i in range(devices)]
+    behind = [(b, a) for a, b in ahead]
+    lower, upper = (lax.ppermute(x, axis, ahead), lax.ppermute(x, axis, behind))
+    made = work(x, here * rows)
+    length = made.shape[out_dim]
+    out = jnp.zeros(
+        (*made.shape[:out_dim], devices * length, *made.shape[out_dim + 1 :]), made.dtype
+    )
+
+    def put(out, made, holder):
+        return lax.dynamic_update_slice_in_dim(out, made, holder * length, axis=out_dim)
+
+    out = put(out, made, here)
+    for hop in range(1, devices // 2 + 1):
+        below, above = ((here - hop) % devices, (here + hop) % devices)
+        held = (lower, upper)
+        if hop < devices // 2:
+            lower, upper = (lax.ppermute(lower, axis, ahead), lax.ppermute(upper, axis, behind))
+        out = put(out, work(held[0], below * rows), below)
+        if 2 * hop < devices:
+            out = put(out, work(held[1], above * rows), above)
+    return out
 
 
 def body(tokens, slot_weight, expert_in, expert_out):
@@ -23,11 +49,14 @@
     experts_here = expert_in.shape[0]
     slot_inputs = (own_rows / own_total[:, None]).astype(jnp.bfloat16)
     slot_inputs = slot_inputs.reshape(experts_here, own_count // experts_here, tokens.shape[1])
-    hidden = jnp.einsum(
-        "esd,edf->esf",
-        lax.all_gather(slot_inputs, "batch", axis=1, tiled=True),
-        expert_in,
-        preferred_element_type=jnp.float32,
+    hidden = on_each_block(
+        slot_inputs,
+        "batch",
+        1,
+        lambda own_block, start: jnp.einsum(
+            "esd,edf->esf", own_block, expert_in, preferred_element_type=jnp.float32
+        ),
+        1,
     )
     hidden = jax.nn.gelu(hidden, approximate=False).astype(jnp.bfloat16)
     terms = jnp.einsum("esf,efd->esd", hidden, expert_out, preferred_element_type=jnp.float32)

time: 167 us -> 167 us (level)
  blocking collectives: 46.5 us -> 27 us
  matrix products: 28.6 us -> 42.3 us
  starting transfers between devices: 0.09 us -> 4.2 us
    all_gather x1 -> x0, blocking collectives: 19.6 us -> none  [body(): lax.all_gather(slot_inputs, 'batch', axis=1, tiled=True)]
    dot_general x1 -> x4, matrix products: 8.12 us -> 21.9 us  [body(): jnp.einsum('esd,edf->esf', own_block, expert_in, preferred_element_type=j...]
    ppermute x0 -> x3, starting transfers between devices: none -> 4.12 us  [the longest x2 3.88 us: on_each_block(): lower, upper = (lax.ppermute(x, axis, ahead), lax.ppermute(x, axis, behind))]
  transfers between devices with their start and end apart: 3 -> 6, of which waited for: 3 -> 3; matrix products, arithmetic and copies ran while one was open for 1% -> 13% of each run, Pallas kernels for 0% -> 0%
where the time goes in v1:
time: 167 us
  waiting for transfers between devices  71.8 us (43%)
  matrix products  42.3 us (25%)
  blocking collectives  27 us (16%)
  between operations  13.3 us (8%)
  other arithmetic  4.83 us (3%)
  starting transfers between devices  4.2 us (3%)
  local copies, waits for them, and re-layouts  3.32 us (2%)
    all_gather x1, waiting for transfers between devices, body(): block_rows = lax.all_gather(slot_outputs, 'token', axis=0, tiled=True)  25.3 us
    reduce_scatter x1, waiting for transfers between devices, body(): lax.psum_scatter(partial_value.astype(jnp.bfloat16), 'token', scatter_dim...  23.5 us
    unnamed x4, waiting for transfers between devices  23 us
    dot_general x4, matrix products, body(): jnp.einsum('esd,edf->esf', own_block, expert_in, preferred_element_type=j...  21.9 us
    pmax x1, blocking collectives, body(): column_max = lax.pmax(jnp.max(logits, axis=0), 'token')  15.2 us
    psum x1, blocking collectives, body(): column_sum = lax.psum(jnp.sum(raised, axis=0), 'token')  11.8 us
    dot_general x1, matrix products, body(): jnp.einsum('esf,efd->esd', hidden, expert_out, preferred_element_type=jnp...  8.93 us
    dot_general x1, matrix products, body(): mixed = jnp.dot(combine, flat_rows, preferred_element_type=jnp.float32)  4 us
  transfers between devices with their start and end apart: 6, of which 3 were waited for; matrix products, arithmetic and copies ran while one was open for 13% of the time, Pallas kernels for 0%

profile of v1, /device:TPU:0, one launch (start us, length us, event | category | flops | bytes accessed | tf_op | source)
XLA Modules:
  0.0 166.7 jit_solution(3083478716375110683)
XLA Ops:
  6.5 1.5 fusion.3
  8.0 0.1 copy-done
  8.2 3.6 %fusion.88 = (f32[512]{0:T(512)S(1)}, f32[1024]{0:T(1024)S(1)}, f32[512,1024]{1,0:T(8,128)}) fusion(bf16[768,1024]{1,0:T(8,128)(2,1)S(1)} %copy-done, bf16[512,768]{1,0:T(8,128)(2,1)} %param.4, f32[512]{0:T(512)S(1)} %add_rsqrt_fusion), kind=kOutput, calls=%fused_computation.105 | convolution fusion | flops 807533056 | bytes 4464640 | tf_op jit(solution)/shard_map/dot_general | solution.py:37
  11.8 15.2 %pmax.7 = f32[1024]{0:T(1024)S(1)} all-reduce(f32[1024]{0:T(1024)S(1)} %get-tuple-element.8), channel_id=1, replica_groups=mesh['batch'=4,'token'=8] {'token'}, use_global_device_ids=true, to_apply=%region_4.0 | all-reduce | flops 1024 | bytes 8192 | tf_op jit(solution)/shard_map/pmax | solution.py:38
  26.9 3.9 %convolution_convert_fusion = bf16[1024,768]{1,0:T(8,128)(2,1)} fusion(f32[512,1024]{1,0:T(8,128)} %get-tuple-element.9, f32[1024]{0:T(1024)S(1)} %pmax.7, bf16[512,768]{1,0:T(8,128)(2,1)S(1)} %copy-done.1, f32[512]{0:T(512)S(1)} %add_rsqrt_fusion), kind=kOutput, calls=%fused_computation.9 | convolution fusion | flops 808321024 | bytes 4462592 | tf_op jit(solution)/shard_map/ts,td->sd/dot_general | solution.py:42
  30.8 0.0 reduce-scatter.5.cloned.1.call-update
  30.8 0.0 reduce-scatter.7.cloned.1.call-start
  30.9 2.3 %fusion = (f32[512]{0:T(512)S(1)}, f32[1024]{0:T(1024)S(1)}) fusion(f32[512,1024]{1,0:T(8,128)} %get-tuple-element.9, f32[512]{0:T(512)S(1)} %get-tuple-element.7, f32[1024]{0:T(1024)S(1)} %pmax.7), kind=kLoop, calls=%fused_computation.6 | loop fusion | flops 2095616 | bytes 2109440 | tf_op jit(solution)/shard_map/reduce_sum | solution.py:66
  33.2 11.8 %psum.7 = f32[1024]{0:T(1024)S(1)} all-reduce(f32[1024]{0:T(1024)S(1)} %get-tuple-element.6), channel_id=1, replica_groups=mesh['batch'=4,'token'=8] {'token'}, use_global_device_ids=true, to_apply=%region_7.8 | all-reduce | flops 1024 | bytes 8192 | tf_op jit(solution)/shard_map/psum | solution.py:40
  45.0 0.1 dynamic_slice.3
  45.1 23.5 %reduce-scatter.5.cloned.1.call-done = bf16[128,768]{1,0:T(8,128)(2,1)} async-done(((bf16[1024,768]{1,0:T(8,128)(2,1)}), bf16[128,768]{1,0:T(8,128)(2,1)}) %reduce-scatter.5.cloned.1.call-update) | async-done | bytes 196624 | tf_op jit(solution)/shard_map/reduce_scatter | solution.py:45
  68.6 1.0 fusion.57
  69.7 1.5 collective-permute-start
  71.2 2.3 %collective-permute-start.1 = (bf16[16,8,768]{2,1,0:T(8,128)(2,1)S(1)}, bf16[16,8,768]{2,1,0:T(8,128)(2,1)S(1)}, u32[]{:S(2)}, u32[]{:S(2)}) collective-permute-start(bf16[16,8,768]{2,1,0:T(8,128)(2,1)S(1)} %fusion.57), channel_id=1, source_target_pairs={{8,0},{16,8},{24,16},{0,24},{9,1},{17,9},{25,17},{1,25},{10,2},{18... | collective-permute-start | bytes 589832 | tf_op jit(solution)/shard_map/ppermute | solution.py:11
  73.6 0.1 broadcast.24
  73.7 8.6 %convolution_dynamic-update-slice_fusion.3 = f32[16,32,768]{2,1,0:T(8,128)S(1)} fusion(f32[16,32,768]{2,1,0:T(8,128)S(1)} %broadcast.24, s32[]{:T(128)S(6)} %select_n.31, bf16[16,8,768]{2,1,0:T(8,128)(2,1)S(1)} %fusion.57, bf16[16,768,768]{2,1,0:T(8,128)(2,1)} %param.6), kind=kOutput, calls=%fused_computation.37 | convolution fusion | flops 150994944 | bytes 19464196 | tf_op jit(solution)/shard_map/esd,edf->esf/dot_general | solution.py:56
  82.3 0.0 collective-permute-done
  82.3 0.2 collective-permute-start.2
  82.6 8.2 %convolution_dynamic-update-slice_fusion.2 = f32[16,32,768]{2,1,0:T(8,128)S(1)} fusion(f32[16,32,768]{2,1,0:T(8,128)S(1)} %convolution_dynamic-update-slice_fusion.3, s32[]{:T(128)S(6)} %select_n.33, bf16[16,8,768]{2,1,0:T(8,128)(2,1)S(1)} %collective-permute-done, bf16[16,768,768]{2,1,0:T(8,128)(2,1)} %param.6), kind=kOutput, calls=%fused_computation.36 | convolution fusion | flops 150994944 | bytes 19464196 | tf_op jit(solution)/shard_map/esd,edf->esf/dot_general | solution.py:56
  90.8 0.3 slice-done.4
  91.1 2.5 %convolution_dynamic-update-slice_fusion.1 = f32[16,32,768]{2,1,0:T(8,128)S(1)} fusion(f32[16,32,768]{2,1,0:T(8,128)S(1)} %convolution_dynamic-update-slice_fusion.2, s32[]{:T(128)S(6)} %select_n.35, bf16[16,8,768]{2,1,0:T(8,128)(2,1)S(1)} %collective-permute-done.1, bf16[16,768,768]{2,1,0:T(8,128)(2,1)S(1)} %bitcast.30), kind=kOutput, calls=%fused_computation.35 | convolution fusion | flops 150994944 | bytes 19464196 | tf_op jit(solution)/shard_map/esd,edf->esf/dot_general | solution.py:56
  93.7 2.5 %convolution_dynamic-update-slice_fusion = f32[16,32,768]{2,1,0:T(8,128)S(1)} fusion(f32[16,32,768]{2,1,0:T(8,128)S(1)} %convolution_dynamic-update-slice_fusion.1, s32[]{:T(128)S(6)} %select_n.37, bf16[16,8,768]{2,1,0:T(8,128)(2,1)S(1)} %collective-permute-done.2, bf16[16,768,768]{2,1,0:T(8,128)(2,1)S(1)} %bitcast.30), kind=kOutput, calls=%fused_computation.34 | convolution fusion | flops 150994944 | bytes 19464196 | tf_op jit(solution)/shard_map/esd,edf->esf/dot_general | solution.py:56
  96.2 8.9 %fusion.89 = bf16[4,8,16,768]{3,1,0,2:T(8,128)(2,1)S(1)} fusion(bf16[16,768,768]{2,1,0:T(8,128)(2,1)} %param.7, f32[16,32,768]{2,1,0:T(8,128)S(1)} %convolution_dynamic-update-slice_fusion), kind=kOutput, calls=%fused_computation.106 | convolution fusion | flops 629932032 | bytes 21233664 | tf_op jit(solution)/shard_map/esf,efd->esd/dot_general | solution.py:62
  105.2 0.9 copy.7
  106.1 0.0 reduce-scatter.7.cloned.1.call-update
  106.1 0.0 all-gather.2.cloned.1.call-start
  106.2 23.0 %reduce-scatter.7.cloned.1.call-done = bf16[8,12288]{1,0:T(8,128)(2,1)} async-done(((bf16[32,12288]{1,0:T(8,128)(2,1)}), bf16[8,12288]{1,0:T(8,128)(2,1)}) %reduce-scatter.7.cloned.1.call-update) | async-done | bytes 196624
  129.1 1.0 copy.11
  130.1 0.7 copy.6
  130.8 0.0 all-gather.2.cloned.1.call-update
  130.9 25.3 %all-gather.2.cloned.1.call-done = bf16[128,8,768]{2,1,0:T(8,128)(2,1)} async-done(((bf16[16,8,768]{2,1,0:T(8,128)(2,1)}), bf16[128,8,768]{2,1,0:T(8,128)(2,1)}) %all-gather.2.cloned.1.call-update) | async-done | bytes 1572880 | tf_op jit(solution)/shard_map/all_gather | solution.py:68
  156.1 4.0 %fusion.17 = bf16[512,768]{1,0:T(8,128)(2,1)} fusion(bf16[128,8,768]{2,1,0:T(8,128)(2,1)} %all-gather.2.cloned.1.call-done, f32[512,1024]{1,0:T(8,128)} %get-tuple-element.9, f32[512]{0:T(512)S(1)} %get-tuple-element.5, f32[512]{0:T(512)S(1)} %get-tuple-element.7), kind=kOutput, calls=%fused_computation.32 | convolution fusion | flops 807272448 | bytes 4460544 | tf_op jit(solution)/shard_map/dot_general | solution.py:71
  (17 shorter events, 0.0 us)
Async XLA Ops:
  6.5 1.6 copy-start
  6.5 62.1 %reduce-scatter.5.cloned.1.call-start = ((), (), s32[]{:S(2)}) async-start(), calls=%async_computation.2 | async-start | bytes 1769472 | tf_op jit(solution)/shard_map/reduce_scatter | solution.py:45
  8.2 18.7 %copy-start.1 = (bf16[512,768]{1,0:T(8,128)(2,1)S(1)}, bf16[512,768]{1,0:T(8,128)(2,1)}, u32[]{:S(2)}) copy-start(bf16[512,768]{1,0:T(8,128)(2,1)} %param.4) | copy-start | bytes 2359300
  30.8 98.3 %reduce-scatter.7.cloned.1.call-start = ((), (), s32[]{:S(2)}) async-start(), calls=%async_computation.4 | async-start | bytes 983040
  69.7 12.7 %collective-permute-start = (bf16[16,8,768]{2,1,0:T(8,128)(2,1)S(1)}, bf16[16,8,768]{2,1,0:T(8,128)(2,1)S(1)}, u32[]{:S(2)}, u32[]{:S(2)}) collective-permute-start(bf16[16,8,768]{2,1,0:T(8,128)(2,1)S(1)} %fusion.57), channel_id=1, source_target_pairs={{0,8},{8,16},{16,24},{24,0},{1,9},{9,17},{17,25},{25,1},{2,10},{10... | collective-permute-start | bytes 589832 | tf_op jit(solution)/shard_map/ppermute | solution.py:11
  71.2 19.6 %collective-permute-start.1 = (bf16[16,8,768]{2,1,0:T(8,128)(2,1)S(1)}, bf16[16,8,768]{2,1,0:T(8,128)(2,1)S(1)}, u32[]{:S(2)}, u32[]{:S(2)}) collective-permute-start(bf16[16,8,768]{2,1,0:T(8,128)(2,1)S(1)} %fusion.57), channel_id=1, source_target_pairs={{8,0},{16,8},{24,16},{0,24},{9,1},{17,9},{25,17},{1,25},{10,2},{18... | collective-permute-start | bytes 589832 | tf_op jit(solution)/shard_map/ppermute | solution.py:11
  73.7 17.1 %slice-start = ((s8[18874368]{0:T(1024)(128)(4,1)}), s8[4194304]{0:T(1024)(128)(4,1)S(1)}, s32[]{:S(2)}) async-start(s8[18874368]{0:T(1024)(128)(4,1)} %bitcast.29), calls=%async_computation.5 | async-start | bytes 8388608
  73.7 17.1 %slice-start.1 = ((s8[18874368]{0:T(1024)(128)(4,1)}), s8[4194304]{0:T(1024)(128)(4,1)S(1)}, s32[]{:S(2)}) async-start(s8[18874368]{0:T(1024)(128)(4,1)} %bitcast.29), calls=%async_computation.6 | async-start | bytes 8388608
  73.7 17.1 %slice-start.2 = ((s8[18874368]{0:T(1024)(128)(4,1)}), s8[4194304]{0:T(1024)(128)(4,1)S(1)}, s32[]{:S(2)}) async-start(s8[18874368]{0:T(1024)(128)(4,1)} %bitcast.29), calls=%async_computation.7 | async-start | bytes 8388608
  82.3 8.5 %slice-start.3 = ((s8[18874368]{0:T(1024)(128)(4,1)}), s8[4194304]{0:T(1024)(128)(4,1)S(1)}, s32[]{:S(2)}) async-start(s8[18874368]{0:T(1024)(128)(4,1)} %bitcast.29), calls=%async_computation.8 | async-start | bytes 8388608
  82.3 8.8 %slice-start.4 = ((s8[18874368]{0:T(1024)(128)(4,1)}), s8[2097152]{0:T(1024)(128)(4,1)S(1)}, s32[]{:S(2)}) async-start(s8[18874368]{0:T(1024)(128)(4,1)} %bitcast.29), calls=%async_computation.9 | async-start | bytes 4194304
  82.3 11.3 %collective-permute-start.2 = (bf16[16,8,768]{2,1,0:T(8,128)(2,1)S(1)}, bf16[16,8,768]{2,1,0:T(8,128)(2,1)S(1)}, u32[]{:S(2)}, u32[]{:S(2)}) collective-permute-start(bf16[16,8,768]{2,1,0:T(8,128)(2,1)S(1)} %collective-permute-done), channel_id=1, source_target_pairs={{0,8},{8,16},{16,24},{24,0},{1,9},{9,17},{17,25},{25,1},{2,10},{10... | collective-permute-start | bytes 589832 | tf_op jit(solution)/shard_map/ppermute | solution.py:26
  106.1 50.0 %all-gather.2.cloned.1.call-start = ((), (), s32[]{:S(2)}) async-start(), calls=%async_computation.3 | async-start | bytes 1769472 | tf_op jit(solution)/shard_map/all_gather | solution.py:68
Sparse Core Ops, SparseCore 0:
  30.9 37.6 reduce-scatter.4
  106.2 22.8 reduce-scatter.6
  131.0 25.0 all-gather.1
